TPU v7x, 32 devices: a whole 2x2x4 slice. The times are simulated.
32 devices in a mesh: cam: 2 (over y), tm: 16 (over z, x, core).
Axes of the slice: x: 2, y: 2, z: 4, core: 2. Of those that a mesh axis runs over, the one named last changes fastest.
Arguments:
- keypoints: int32 [4, 34, 8192], P('cam', None, 'tm'), may hold values from 0 to 4095
- visibility: int32 [4, 8192], P(None, 'tm'), may hold values 0 or 1
- expand_weight: bfloat16 [3, 34, 1024], replicated, may hold values from -0.625 to 0.625
- dilated_tap_weight: bfloat16 [1024, 3, 1024], P('tm'), may hold values from -0.109375 to 0.109375
- join_weight: bfloat16 [1024, 64], replicated, may hold values from -0.1875 to 0.1875
- decay_rates: float32 [64, 8192], P('cam', 'tm'), may hold values from 0 to 1, as said below
Outputs:
- smoothed: float32 [64, 8192], P('cam', 'tm')
Inputs may be any that keep to these rules, and one draw needn't show every extreme that they name: `keypoints`: quantized image coordinates. `decay_rates`: positive rates.
All inputs are finite; a program needn't handle non-finite values. No bound on the sum of `visibility` on one device may be relied on, other than what follows from the above.
Results may differ from a plain program's by a relative error of at most 0.00045.
Values may be sent and summed in bfloat16 or wider, within the bound.
A program may use at most 64 MiB of HBM per device.

v0:
```python
import functools

import jax
import jax.numpy as jnp
from jax import lax
from jax.experimental import pallas as pl
from jax.experimental.pallas import tpu as pltpu
from jax.sharding import PartitionSpec as P

DILATION_STEP = 3
MESH = pl.DeviceIdType.MESH


def with_halo(array, sides, width):
    for axis, dim in sides:
        count, length = (lax.axis_size(axis), array.shape[dim])
        up = [(i, (i + 1) % count) for i in range(count - 1)]
        down = [(j, i) for i, j in up]
        last = lax.slice_in_dim(array, length - width, length, axis=dim)
        initial = lax.slice_in_dim(array, 0, width, axis=dim)
        before = lax.ppermute(last, axis, up)
        after = lax.ppermute(initial, axis, down)
        array = jnp.concatenate([before, array, after], axis=dim)
    return array


def entering(part, axis, combine, identity, reverse):
    count = lax.axis_size(axis)
    place = lax.axis_index(axis)
    ahead = count - 1 - place if reverse else place
    gathered = jax.tree.map(lambda a: lax.all_gather(a, axis), part)
    state = jax.tree.map(lambda a, e: jnp.zeros_like(a) + jnp.asarray(e, a.dtype), part, identity)

    def one(turn, state):
        source = count - 1 - turn if reverse else turn
        return combine(
            state, jax.tree.map(lambda a: lax.dynamic_index_in_dim(a, source, 0, False), gathered)
        )

    return lax.fori_loop(0, ahead, one, state)


def expand(widened_output, expand_weight, width):
    total = None
    for shift_amount in range(3):
        term = jnp.einsum(
            "vjt,jc->vtc",
            widened_output[:, :, shift_amount : shift_amount + width],
            expand_weight[shift_amount],
            preferred_element_type=jnp.float32,
        )
        total = term if total is None else total + term
    return jax.nn.relu(total).astype(jnp.bfloat16)


def dilate(padded_input, hidden_start0, weight_rows):
    count_of_frames = hidden_start0.shape[1]
    total = None
    for shift_amount in range(3):
        term = jnp.einsum(
            "vti,ni->vtn",
            padded_input[
                :, shift_amount * DILATION_STEP : shift_amount * DILATION_STEP + count_of_frames
            ],
            weight_rows[:, shift_amount],
            preferred_element_type=jnp.float32,
        )
        total = term if total is None else total + term
    residual = hidden_start0.astype(jnp.float32)
    return (residual + jax.nn.relu(total)).astype(jnp.bfloat16)


def chain(earlier, latter):
    return (earlier[0] * latter[0], latter[0] * earlier[1] + latter[1])


def body(keypoints, visibility, expand_weight, dilated_tap_weight, join_weight, decay_rates):
    view_count = keypoints.shape[0]
    count_of_frames = keypoints.shape[2]
    coords = ((keypoints.astype(jnp.float32) - 2048.0) / 2048.0).astype(jnp.bfloat16)
    widened_output = with_halo(coords, (("tm", 2),), 1)
    hidden_start0 = expand(widened_output, expand_weight, count_of_frames)
    padded_input = with_halo(hidden_start0, (("tm", 1),), DILATION_STEP)
    hidden1 = dilate(
        padded_input, hidden_start0, lax.all_gather(dilated_tap_weight, "tm", axis=0, tiled=True)
    )
    own_mask = lax.dynamic_slice_in_dim(
        visibility, lax.axis_index("cam") * view_count, view_count, 0
    )
    masked = hidden1 * own_mask[:, :, None].astype(jnp.bfloat16)
    state_rows = decay_rates.shape[0]
    total = lax.psum_scatter(
        jnp.einsum("vti,is->st", masked, join_weight, preferred_element_type=jnp.float32).astype(
            jnp.bfloat16
        ),
        "cam",
        scatter_dimension=0,
        tiled=True,
    ).astype(jnp.float32)
    seen = jnp.sum(visibility.astype(jnp.float32), axis=0)
    joined = total / jnp.maximum(seen, 1.0)[None, :]
    decay = jnp.exp(-decay_rates)
    energy = -jnp.expm1(-2.0 * decay_rates)
    drive = jnp.sqrt(energy)
    prod_fwd, local_fwd = lax.associative_scan(chain, (decay, drive * joined), axis=1)
    ones_vec = jnp.ones((state_rows,), jnp.float32)
    zeros_vec = jnp.zeros((state_rows,), jnp.float32)
    carried = entering(
        (prod_fwd[:, -1], local_fwd[:, -1]), "tm", chain, (ones_vec, zeros_vec), False
    )
    filtered = local_fwd + prod_fwd * carried[1][:, None]
    prod_back, local_back = lax.associative_scan(
        chain, (decay, energy * filtered), axis=1, reverse=True
    )
    returned = entering(
        (prod_back[:, 0], local_back[:, 0]), "tm", chain, (ones_vec, zeros_vec), True
    )
    smoothed = local_back + prod_back * returned[1][:, None]
    return smoothed

SIDE = 128
DEPTH = 48
LANES = 128


def neg_expm1(u):
    series = jnp.ones_like(u)
    for k in range(11, 1, -1):
        series = 1.0 - series * u * (1.0 / k)
    return jnp.where(u < 0.5, u * series, 1.0 - jnp.exp(-u))


def block_kernel(
    cams, layers, group, keys_ref, vis_ref, first_ref, taps_ref, join_ref, rates_ref, out_ref,
    coords, hidden, mixed, weights, stage, part_out, part_in, ends,
    coord_send, coord_recv, side_send, side_recv, up_send, down_send, tap_recv,
    part_send, part_recv, end_send, end_recv,
):
    views, joints, length = keys_ref.shape
    channels = first_ref.shape[0]
    count = layers * group
    all_cams = cams * views
    rows = taps_ref.shape[1] // cams
    own = layers * rows
    states = rates_ref.shape[0]
    all_states = join_ref.shape[1]
    members = group * cams
    span = group * length
    f32, bf16 = jnp.float32, jnp.bfloat16
    y = lax.axis_index("cam")
    i = lax.axis_index("tm")
    z = i // group
    l = i % group
    me = l * cams + y

    barrier = pltpu.get_barrier_semaphore()
    everyone = cams * count
    flat = i * cams + y

    @pl.loop(1, everyone)
    def _(d):
        other = lax.rem(flat + d, everyone)
        pl.semaphore_signal(
            barrier, inc=1, device_id=(other % cams, other // cams), device_id_type=MESH
        )

    here = pl.ds(pl.multiple_of(SIDE + l * length, LANES), length)
    for v in range(views):
        stage[...] = jnp.zeros_like(stage)
        stage[pl.ds(0, joints), :] = (keys_ref[v].astype(f32) - 2048.0) / 2048.0
        stage[pl.ds(joints, 1), :] = vis_ref[pl.ds(y * views + v, 1), :].astype(f32)
        coords[y * views + v, :, here] = stage[...].astype(bf16)

    @pl.when(z == 0)
    def _():
        coords[:, :, 0:SIDE] = jnp.zeros((all_cams, DEPTH, SIDE), bf16)

    @pl.when(z == layers - 1)
    def _():
        coords[:, :, SIDE + span : SIDE + span + SIDE] = jnp.zeros((all_cams, DEPTH, SIDE), bf16)

    pl.semaphore_wait(barrier, everyone - 1)

    def tap_copy(source, target, sem, first):
        src = taps_ref.at[:, pl.ds(pl.multiple_of(y * rows, rows), rows), :]
        if not first:
            src = weights.at[pl.ds(0, 3), source]
        return pltpu.make_async_remote_copy(
            src_ref=src,
            dst_ref=weights.at[pl.ds(0, 3), source],
            send_sem=sem.at[source],
            recv_sem=tap_recv.at[source],
            device_id=(y, target * group + l),
            device_id_type=MESH,
        )

    def pass_on(source, upward, first):
        if upward:
            @pl.when(z < layers - 1)
            def _():
                tap_copy(source, z + 1, up_send, first).start()
        else:
            @pl.when(z > 0)
            def _():
                tap_copy(source, z - 1, down_send, first).start()

    def arrive(hop):
        @pl.when(z >= hop)
        def _():
            tap_copy(z - hop, z, up_send, False).wait_recv()
            if hop < layers - 1:
                pass_on(z - hop, True, False)

        @pl.when(z + hop < layers)
        def _():
            tap_copy(z + hop, z, down_send, False).wait_recv()
            if hop < layers - 1:
                pass_on(z + hop, False, False)

    def side_copy(side, sender, target, sem):
        cam_rows = pl.ds(sender * views, views)
        if side == 0:
            src, dst = pl.ds(span, SIDE), pl.ds(0, SIDE)
        else:
            src, dst = pl.ds(SIDE, SIDE), pl.ds(SIDE + span, SIDE)
        return pltpu.make_async_remote_copy(
            src_ref=coords.at[cam_rows, :, src],
            dst_ref=coords.at[cam_rows, :, dst],
            send_sem=sem,
            recv_sem=side_recv.at[side * cams + sender],
            device_id=target,
            device_id_type=MESH,
        )

    def coord_copy(sender, target, sem):
        lanes = pl.ds(pl.multiple_of(SIDE + (sender // cams) * length, LANES), length)
        at = coords.at[pl.ds((sender % cams) * views, views), :, lanes]
        return pltpu.make_async_remote_copy(
            src_ref=at,
            dst_ref=at,
            send_sem=sem,
            recv_sem=coord_recv.at[sender],
            device_id=(target % cams, z * group + target // cams),
            device_id_type=MESH,
        )

    pass_on(z, True, True)
    pass_on(z, False, True)

    for d in range(1, members):
        target = lax.rem(me + d, members)
        coord_copy(me, target, coord_send.at[target]).start()

    @pl.when((l == group - 1) & (z < layers - 1))
    def _():
        for p in range(members):
            side_copy(0, y, (p % cams, (z + 1) * group + p // cams), side_send.at[p]).start()

    @pl.when((l == 0) & (z > 0))
    def _():
        for p in range(members):
            side_copy(1, y, (p % cams, (z - 1) * group + p // cams), side_send.at[p]).start()

    for o in range(3):
        weights[o, z] = taps_ref[o, pl.ds(pl.multiple_of(y * rows, rows), rows), :]
    for s in range(layers):
        base = (s * group + l) * (rows * cams) + y * rows
        r = lax.broadcasted_iota(jnp.int32, (rows, channels), 0)
        c = lax.broadcasted_iota(jnp.int32, (rows, channels), 1)
        weights[3, s] = jnp.where(c == r + base, 1.0, 0.0).astype(bf16)

    lane = lax.broadcasted_iota(jnp.int32, (states, length), 1)

    def scan(prod, values, reverse):
        step = 1
        while step < length:
            turn = length - step if reverse else step
            fits = (lane < length - step) if reverse else (lane >= step)
            values = [
                val + prod * jnp.where(fits, pltpu.roll(val, turn, 1), 0.0) for val in values
            ]
            prod = prod * jnp.where(fits, pltpu.roll(prod, turn, 1), 1.0)
            step *= 2
        return prod, values

    for d in range(1, members):
        source = lax.rem(me + members - d, members)
        coord_copy(source, source, coord_send.at[source]).wait_recv()

    @pl.when(z > 0)
    def _():
        for p in range(cams):
            side_copy(0, p, (y, i), side_send.at[p]).wait_recv()

    @pl.when(z < layers - 1)
    def _():
        for p in range(cams):
            side_copy(1, p, (y, i), side_send.at[p]).wait_recv()

    def expand_block(v, start, width):
        wide = coords[v, :, pl.ds(start - SIDE, width + 2 * SIDE)].astype(f32)
        full = width + 2 * SIDE
        x = jnp.concatenate(
            [
                pltpu.roll(wide, 1, 1)[:, SIDE : SIDE + width],
                wide[:, SIDE : SIDE + width],
                pltpu.roll(wide, full - 1, 1)[:, SIDE : SIDE + width],
            ],
            axis=0,
        ).astype(bf16)
        return jnp.maximum(jnp.dot(first_ref[...], x, preferred_element_type=f32), 0.0)

    def expand_some(begin, end):
        @pl.loop(begin, end)
        def _(n):
            v, s = n // group, n % group
            start = pl.multiple_of(SIDE + s * length, LANES)
            hidden[n] = expand_block(v, start, length).astype(bf16)

    whole = all_cams * group
    expand_some(0, whole // 4)
    arrive(1)
    expand_some(whole // 4, whole // 2)
    for hop in range(2, layers - 1):
        arrive(hop)
    expand_some(whole // 2, whole)

    slab = lax.broadcasted_iota(jnp.int32, (DEPTH, SIDE), 1)
    low = slab < SIDE // 2
    wide_slab = lax.broadcasted_iota(jnp.int32, (channels, SIDE), 1)
    keep = ((wide_slab < SIDE // 2) & (z < layers - 1)) | ((wide_slab >= SIDE // 2) & (z > 0))
    for v in range(all_cams):
        before = coords[v, :, 0:SIDE].astype(f32)
        begin = coords[v, :, SIDE : 2 * SIDE].astype(f32)
        end = coords[v, :, span : SIDE + span].astype(f32)
        after = coords[v, :, SIDE + span : SIDE + span + SIDE].astype(f32)
        older = jnp.where(slab == 0, pltpu.roll(end, 1, 1), pltpu.roll(after, 1, 1))
        newer = jnp.where(
            slab == SIDE - 1, pltpu.roll(begin, SIDE - 1, 1), pltpu.roll(before, SIDE - 1, 1)
        )
        x = jnp.concatenate(
            [
                jnp.where(low, older, pltpu.roll(before, 1, 1)),
                jnp.where(low, after, before),
                jnp.where(low, pltpu.roll(after, SIDE - 1, 1), newer),
            ],
            axis=0,
        ).astype(bf16)
        h = jnp.maximum(jnp.dot(first_ref[...], x, preferred_element_type=f32), 0.0)
        hidden[whole, :, v * SIDE : (v + 1) * SIDE] = jnp.where(keep, h, 0.0).astype(bf16)

    rates = rates_ref[...]
    decay = jnp.exp(-rates)
    energy = neg_expm1(2.0 * rates)
    drive = jnp.sqrt(energy)

    arrive(layers - 1)
    stack = weights[...].reshape(4 * own, channels)

    z_slab = jnp.dot(stack, hidden[whole], preferred_element_type=f32)
    for v in range(all_cams):
        piece = z_slab[:, v * SIDE : (v + 1) * SIDE]
        mixed[v, :, 0:SIDE] = piece
        mixed[v, :, SIDE + span : SIDE + span + SIDE] = piece

    @pl.loop(0, whole)
    def _(n):
        v, s = n // group, n % group
        lanes = pl.ds(pl.multiple_of(SIDE + s * length, LANES), length)
        mixed[v, :, lanes] = jnp.dot(
            weights[...].reshape(4 * own, channels), hidden[n], preferred_element_type=f32
        )

    picked = jnp.concatenate(
        [
            join_ref[pl.ds(pl.multiple_of((s * group + l) * (rows * cams) + y * rows, rows), rows), :]
            for s in range(layers)
        ],
        axis=0,
    )
    twice = jnp.concatenate([picked, picked], axis=0)

    def part_copy(slot, source, target, sem):
        return pltpu.make_async_remote_copy(
            src_ref=part_out.at[slot],
            dst_ref=part_in.at[source],
            send_sem=sem,
            recv_sem=part_recv.at[source],
            device_id=(target % cams, z * group + target // cams),
            device_id_type=MESH,
        )

    for d in range(group):
        s = lax.rem(l + d + 1, group)
        centre = pl.ds(pl.multiple_of(SIDE + s * length, LANES), length)
        earlier = pl.ds(pl.multiple_of(s * length, LANES), SIDE + length)
        later = pl.ds(pl.multiple_of(SIDE + s * length, LANES), SIDE + length)
        total = jnp.zeros((own, length), f32)
        for v in range(all_cams):
            left = pltpu.roll(mixed[v, 0:own, earlier], DILATION_STEP, 1)[:, SIDE:]
            right = pltpu.roll(
                mixed[v, 2 * own : 3 * own, later], SIDE + length - DILATION_STEP, 1
            )[:, :length]
            acc = left + mixed[v, own : 2 * own, centre] + right
            h = (mixed[v, 3 * own : 4 * own, centre] + jnp.maximum(acc, 0.0)).astype(bf16)
            mask = coords[v, :, centre].astype(f32)[joints : joints + 1, :]
            total = total + h.astype(f32) * mask
        top = total.astype(bf16)
        rest = (total - top.astype(f32)).astype(bf16)
        both = jnp.concatenate([top, rest], axis=0)
        result = lax.dot_general(
            twice, both, (((0,), (0,)), ((), ())), preferred_element_type=f32
        ).astype(bf16)
        for p in range(cams):
            part_out[s * cams + p] = result[p * states : (p + 1) * states]
        for p in range(cams):
            target = s * cams + p
            if d < group - 1:
                part_copy(target, me, target, part_send.at[target]).start()
            else:
                @pl.when(p != y)
                def _():
                    part_copy(target, me, target, part_send.at[target]).start()

                @pl.when(p == y)
                def _():
                    part_in[me] = part_out[target]

    seen = jnp.sum(vis_ref[...].astype(f32), axis=0, keepdims=True)
    for d in range(1, members):
        source = lax.rem(me + members - d, members)
        part_copy(source, source, source, part_send.at[source]).wait_recv()
    summed = part_in[0].astype(f32)
    for p in range(1, members):
        summed = summed + part_in[p].astype(f32)
    joined = summed / jnp.maximum(seen, 1.0)

    prod_fwd, (local,) = scan(decay, [drive * joined], False)
    prod_back, (back, through) = scan(decay, [energy * local, energy * prod_fwd], True)

    square = lax.broadcasted_iota(jnp.int32, (states, LANES), 1)
    packed = jnp.where(
        square == 0,
        prod_fwd[:, length - 1 : length],
        jnp.where(
            square == 1,
            local[:, length - 1 : length],
            jnp.where(square == 2, back[:, 0:1], through[:, 0:1]),
        ),
    )
    packed = jnp.concatenate([packed, jnp.zeros((LANES - states, LANES), f32)], axis=0)
    ends[i] = packed.T[0:8]

    def end_copy(source, target, sem):
        return pltpu.make_async_remote_copy(
            src_ref=ends.at[source],
            dst_ref=ends.at[source],
            send_sem=sem,
            recv_sem=end_recv.at[source],
            device_id=(y, target),
            device_id_type=MESH,
        )

    for d in range(1, count):
        target = lax.rem(i + d, count)
        end_copy(i, target, end_send.at[target]).start()
    for d in range(1, count):
        source = lax.rem(i + count - d, count)
        end_copy(source, source, end_send.at[source]).wait_recv()

    entry = jnp.zeros((1, LANES), f32)
    carried = entry
    entries = []
    for j in range(count):
        entries.append(entry)
        carried = jnp.where(j == i, entry, carried)
        entry = ends[j, 0:1] * entry + ends[j, 1:2]
    state = jnp.zeros((1, LANES), f32)
    returned = state
    for j in range(count - 1, -1, -1):
        returned = jnp.where(j == i, state, returned)
        state = ends[j, 0:1] * state + ends[j, 2:3] + ends[j, 3:4] * entries[j]
    both = jnp.concatenate([carried, returned, jnp.zeros((LANES - 2, LANES), f32)], axis=0).T
    out_ref[...] = back + through * both[0:states, 0:1] + prod_back * both[0:states, 1:2]

    for d in range(1, members):
        target = lax.rem(me + d, members)
        coord_copy(me, target, coord_send.at[target]).wait_send()
        part_copy(target, me, target, part_send.at[target]).wait_send()
    for d in range(1, count):
        target = lax.rem(i + d, count)
        end_copy(i, target, end_send.at[target]).wait_send()

    @pl.when((l == group - 1) & (z < layers - 1))
    def _():
        for p in range(members):
            side_copy(0, y, (p % cams, (z + 1) * group + p // cams), side_send.at[p]).wait_send()

    @pl.when((l == 0) & (z > 0))
    def _():
        for p in range(members):
            side_copy(1, y, (p % cams, (z - 1) * group + p // cams), side_send.at[p]).wait_send()

    for hop in range(layers - 1):
        @pl.when((z < layers - 1) & (z - hop >= 0))
        def _():
            tap_copy(z - hop, z + 1, up_send, hop == 0).wait_send()

        @pl.when((z > 0) & (z + hop < layers))
        def _():
            tap_copy(z + hop, z - 1, down_send, hop == 0).wait_send()


def block_body(cams, count, group):
    layers = count // group

    def run(keypoints, visibility, expand_weight, dilated_tap_weight, join_weight, decay_rates):
        views, joints, length = keypoints.shape
        channels = expand_weight.shape[2]
        rows = dilated_tap_weight.shape[0] // cams
        own = layers * rows
        members = group * cams
        all_cams = cams * views
        states = decay_rates.shape[0]
        first = jnp.pad(expand_weight, ((0, 0), (0, DEPTH - joints), (0, 0)))
        first = first.reshape(3 * DEPTH, channels).T
        taps = jnp.transpose(dilated_tap_weight, (1, 0, 2))
        extended = group * length + 2 * SIDE
        dma, vmem, bf16 = (pltpu.SemaphoreType.DMA, pltpu.VMEM, jnp.bfloat16)
        return pl.pallas_call(
            functools.partial(block_kernel, cams, layers, group),
            out_shape=jax.ShapeDtypeStruct(decay_rates.shape, jnp.float32),
            in_specs=[pl.BlockSpec(memory_space=pltpu.VMEM)] * 6,
            out_specs=pl.BlockSpec(memory_space=pltpu.VMEM),
            scratch_shapes=[
                vmem((all_cams, DEPTH, extended), bf16),
                vmem((all_cams * group + 1, channels, length), bf16),
                vmem((all_cams, 4 * own, extended), jnp.float32),
                vmem((4, layers, rows, channels), bf16),
                vmem((DEPTH, length), jnp.float32),
                vmem((members, states, length), bf16),
                vmem((members, states, length), bf16),
                vmem((count, 8, LANES), jnp.float32),
                dma((members,)),
                dma((members,)),
                dma((members,)),
                dma((2 * cams,)),
                dma((layers,)),
                dma((layers,)),
                dma((layers,)),
                dma((members,)),
                dma((members,)),
                dma((count,)),
                dma((count,)),
            ],
            compiler_params=pltpu.CompilerParams(
                collective_id=0, has_side_effects=True, vmem_limit_bytes=58 * 1024 * 1024
            ),
        )(keypoints, visibility, first, taps, join_weight, decay_rates)

    return run


def solution(mesh):
    cams, count = mesh.shape["cam"], mesh.shape["tm"]
    group = 4
    fits = count % group == 0 and cams == 2 and count == 4 * group
    return jax.shard_map(
        block_body(cams, count, group) if fits else body,
        mesh=mesh,
        in_specs=(
            P("cam", None, "tm"),
            P(None, "tm"),
            P(),
            P("tm", None, None),
            P(),
            P("cam", "tm"),
        ),
        out_specs=P("cam", "tm"),
        check_vma=False,
    )
```

profile of v0, /device:TPU:0, one launch (start us, length us, event | category | flops | bytes accessed | tf_op | source)
XLA Modules:
  0.0 61.9 jit_solution(11272603147610659019)
XLA Ops:
  0.0 1.0 %pad.4 = bf16[3,48,1024]{2,1,0:T(8,128)(2,1)S(1)} pad(bf16[3,34,1024]{2,1,0:T(8,128)(2,1)} %param.8, bf16[]{:T(256)} %constant.2.clone.1), padding=0_0x0_14x0_0 | pad | bytes 503810 | tf_op jit(solution)/shard_map/jit(_pad)/pad | solution.py:525
  1.0 0.0 copy-start.1
  1.0 1.0 %copy.10 = bf16[144,1024]{0,1:T(8,128)(2,1)} copy(bf16[144,1024]{1,0:T(8,128)(2,1)S(1)} %bitcast.4) | data formatting | bytes 589824 | tf_op jit(solution)/shard_map/reshape | solution.py:526
  2.0 0.0 copy-done.1
  2.0 0.0 copy-start
  2.0 0.8 %copy.12.join_ref = bf16[1024,64]{1,0:T(8,128)(2,1)} copy(bf16[1024,64]{0,1:T(8,128)(2,1)S(1)} %copy-done.1) | data formatting | bytes 262144 | tf_op args[4]
  2.8 0.1 copy-done
  2.9 0.7 %copy.11.keys_ref = s32[2,34,512]{2,1,0:T(8,128)} copy(s32[2,34,512]{2,0,1:T(2,128)S(1)} %copy-done) | data formatting | bytes 278528 | tf_op args[0]
  3.6 56.8 %shard_map.64 = f32[32,512]{1,0:T(8,128)} custom-call(s32[2,34,512]{2,1,0:T(8,128)} %copy.11.keys_ref, s32[4,512]{1,0:T(4,128)} %vis_ref.1, bf16[1024,144]{1,0:T(8,128)(2,1)} %bitcast.3, bf16[3,64,1024]{2,1,0:T(8,128)(2,1)} %bitcast.5, bf16[1024,64]{1,0:T(8,128)(2,1)} %copy.12.join_ref, f32[32,512]{1,0:T(8,128)} %rates_ref.1), custom_call_target="tpu_custom_call" | custom-call | tf_op jit(solution)/shard_map/pallas_call | solution.py:530
  60.4 1.5 %copy.14 = f32[32,512]{1,0:T(8,128)} copy(f32[32,512]{1,0:T(8,128)} %shard_map.64) | data formatting | bytes 131072
Async XLA Ops:
  1.0 1.0 %copy-start.1 = (bf16[1024,64]{0,1:T(8,128)(2,1)S(1)}, bf16[1024,64]{0,1:T(8,128)(2,1)}, u32[]{:S(2)}) copy-start(bf16[1024,64]{0,1:T(8,128)(2,1)} %param.10) | copy-start | bytes 393220
  2.0 0.9 %copy-start = (s32[2,34,512]{2,0,1:T(2,128)S(1)}, s32[2,34,512]{2,0,1:T(2,128)}, u32[]{:S(2)}) copy-start(s32[2,34,512]{2,0,1:T(2,128)} %param.6) | copy-start | bytes 417796
where the time goes:
time: 62.1 us; the launch traced here: 61.9 us
  Pallas kernels  56.8 us (91%)
  local copies, waits for them, and re-layouts  5.03 us (8%)
    pallas_call x1, Pallas kernels, run(): pl.pallas_call(functools.partial(block_kernel, cams, layers, group), out_...  56.8 us
    unnamed x7, local copies, waits for them, and re-layouts  3.08 us

commit v1 on v0

--- a/solution.py
+++ b/solution.py
@@ -119,7 +119,7 @@
     return smoothed
 
 SIDE = 128
-DEPTH = 48
+DEPTH = 40
 LANES = 128
 
 
@@ -131,19 +131,18 @@
 
 
 def block_kernel(
-    cams, layers, group, keys_ref, vis_ref, first_ref, taps_ref, join_ref, rates_ref, out_ref,
-    coords, hidden, mixed, weights, stage, part_out, part_in, ends,
-    coord_send, coord_recv, side_send, side_recv, up_send, down_send, tap_recv,
+    cams, layers, group, keys_ref, vis_ref, raw_ref, taps_ref, join_ref, rates_ref, out_ref,
+    first_wide, first_ref, coords, hidden, mixed, weights, stack, stage, part_out, part_in, ends,
+    coord_send, coord_recv, relay_send, side_send, side_recv, up_send, down_send, tap_recv,
     part_send, part_recv, end_send, end_recv,
 ):
-    views, joints, length = keys_ref.shape
-    channels = first_ref.shape[0]
+    joints, views, length = keys_ref.shape
+    channels = raw_ref.shape[2]
     count = layers * group
     all_cams = cams * views
     rows = taps_ref.shape[1] // cams
     own = layers * rows
     states = rates_ref.shape[0]
-    all_states = join_ref.shape[1]
     members = group * cams
     span = group * length
     f32, bf16 = jnp.float32, jnp.bfloat16
@@ -167,7 +166,7 @@
     here = pl.ds(pl.multiple_of(SIDE + l * length, LANES), length)
     for v in range(views):
         stage[...] = jnp.zeros_like(stage)
-        stage[pl.ds(0, joints), :] = (keys_ref[v].astype(f32) - 2048.0) / 2048.0
+        stage[pl.ds(0, joints), :] = (keys_ref[:, v, :].astype(f32) - 2048.0) / 2048.0
         stage[pl.ds(joints, 1), :] = vis_ref[pl.ds(y * views + v, 1), :].astype(f32)
         coords[y * views + v, :, here] = stage[...].astype(bf16)
 
@@ -178,6 +177,30 @@
     @pl.when(z == layers - 1)
     def _():
         coords[:, :, SIDE + span : SIDE + span + SIDE] = jnp.zeros((all_cams, DEPTH, SIDE), bf16)
+
+    first_wide[...] = jnp.zeros_like(first_wide)
+    for o in range(3):
+        first_wide[pl.ds(o * DEPTH, joints), :] = raw_ref[o].astype(f32)
+    first_ref[...] = first_wide[...].T[:, : 3 * DEPTH].astype(bf16)
+
+    for o in range(3):
+        weights[o, z] = taps_ref[o, pl.ds(pl.multiple_of(y * rows, rows), rows), :]
+    for s in range(layers):
+        base = (s * group + l) * (rows * cams) + y * rows
+        r = lax.broadcasted_iota(jnp.int32, (rows, channels), 0)
+        c = lax.broadcasted_iota(jnp.int32, (rows, channels), 1)
+        weights[3, s] = jnp.where(c == r + base, 1.0, 0.0).astype(bf16)
+    near = jnp.where(z < layers - 1, z + 1, z - 1)
+    far = jnp.where(z == 0, 2, 0)
+    last = jnp.where(z < 2, 3, 1)
+    halves = ((z, near), (far, last))
+    picked = lax.dot_general(
+        join_ref[...],
+        jnp.concatenate([weights[3, t] for pair in halves for t in pair], axis=0),
+        (((1,), (1,)), ((), ())),
+        preferred_element_type=f32,
+    ).astype(bf16)
+    twice = jnp.concatenate([picked, picked], axis=1)
 
     pl.semaphore_wait(barrier, everyone - 1)
 
@@ -247,8 +270,17 @@
     pass_on(z, True, True)
     pass_on(z, False, True)
 
-    for d in range(1, members):
-        target = lax.rem(me + d, members)
+    turns = [(a, b) for a in range(group // 2) for b in range(cams) if a + b > 0]
+    core = l % 2
+    mate = (l + 1 - 2 * core) * cams + y
+
+    def alike(a, b, side):
+        chip = lax.rem(l // 2 + a, group // 2)
+        return (chip * 2 + side) * cams + lax.rem(y + b, cams)
+
+    coord_copy(me, mate, coord_send.at[mate]).start()
+    for a, b in turns:
+        target = alike(a, b, core)
         coord_copy(me, target, coord_send.at[target]).start()
 
     @pl.when((l == group - 1) & (z < layers - 1))
@@ -260,14 +292,6 @@
     def _():
         for p in range(members):
             side_copy(1, y, (p % cams, (z - 1) * group + p // cams), side_send.at[p]).start()
-
-    for o in range(3):
-        weights[o, z] = taps_ref[o, pl.ds(pl.multiple_of(y * rows, rows), rows), :]
-    for s in range(layers):
-        base = (s * group + l) * (rows * cams) + y * rows
-        r = lax.broadcasted_iota(jnp.int32, (rows, channels), 0)
-        c = lax.broadcasted_iota(jnp.int32, (rows, channels), 1)
-        weights[3, s] = jnp.where(c == r + base, 1.0, 0.0).astype(bf16)
 
     lane = lax.broadcasted_iota(jnp.int32, (states, length), 1)
 
@@ -283,8 +307,13 @@
             step *= 2
         return prod, values
 
-    for d in range(1, members):
-        source = lax.rem(me + members - d, members)
+    for a, b in turns:
+        source = alike(a, b, core)
+        coord_copy(source, source, coord_send.at[source]).wait_recv()
+        coord_copy(source, mate, relay_send.at[source]).start()
+    arrive(1)
+    for a, b in [(0, 0)] + turns:
+        source = alike(a, b, 1 - core)
         coord_copy(source, source, coord_send.at[source]).wait_recv()
 
     @pl.when(z > 0)
@@ -318,12 +347,10 @@
             hidden[n] = expand_block(v, start, length).astype(bf16)
 
     whole = all_cams * group
-    expand_some(0, whole // 4)
-    arrive(1)
-    expand_some(whole // 4, whole // 2)
+    expand_some(0, 3 * whole // 4)
     for hop in range(2, layers - 1):
         arrive(hop)
-    expand_some(whole // 2, whole)
+    expand_some(3 * whole // 4, whole)
 
     slab = lax.broadcasted_iota(jnp.int32, (DEPTH, SIDE), 1)
     low = slab < SIDE // 2
@@ -354,31 +381,29 @@
     energy = neg_expm1(2.0 * rates)
     drive = jnp.sqrt(energy)
 
+    half = own // 2
+
+    def mix(part):
+        stack[...] = jnp.concatenate(
+            [weights[o, t] for o in range(4) for t in halves[part]], axis=0
+        )
+        z_slab = jnp.dot(stack[...], hidden[whole], preferred_element_type=f32)
+        for v in range(all_cams):
+            piece = z_slab[:, v * SIDE : (v + 1) * SIDE]
+            mixed[v, part, :, 0:SIDE] = piece
+            mixed[v, part, :, SIDE + span : SIDE + span + SIDE] = piece
+
+        @pl.loop(0, whole)
+        def _(n):
+            v, s = n // group, n % group
+            lanes = pl.ds(pl.multiple_of(SIDE + s * length, LANES), length)
+            mixed[v, part, :, lanes] = jnp.dot(
+                stack[...], hidden[n], preferred_element_type=f32
+            )
+
+    mix(0)
     arrive(layers - 1)
-    stack = weights[...].reshape(4 * own, channels)
-
-    z_slab = jnp.dot(stack, hidden[whole], preferred_element_type=f32)
-    for v in range(all_cams):
-        piece = z_slab[:, v * SIDE : (v + 1) * SIDE]
-        mixed[v, :, 0:SIDE] = piece
-        mixed[v, :, SIDE + span : SIDE + span + SIDE] = piece
-
-    @pl.loop(0, whole)
-    def _(n):
-        v, s = n // group, n % group
-        lanes = pl.ds(pl.multiple_of(SIDE + s * length, LANES), length)
-        mixed[v, :, lanes] = jnp.dot(
-            weights[...].reshape(4 * own, channels), hidden[n], preferred_element_type=f32
-        )
-
-    picked = jnp.concatenate(
-        [
-            join_ref[pl.ds(pl.multiple_of((s * group + l) * (rows * cams) + y * rows, rows), rows), :]
-            for s in range(layers)
-        ],
-        axis=0,
-    )
-    twice = jnp.concatenate([picked, picked], axis=0)
+    mix(1)
 
     def part_copy(slot, source, target, sem):
         return pltpu.make_async_remote_copy(
@@ -395,22 +420,24 @@
         centre = pl.ds(pl.multiple_of(SIDE + s * length, LANES), length)
         earlier = pl.ds(pl.multiple_of(s * length, LANES), SIDE + length)
         later = pl.ds(pl.multiple_of(SIDE + s * length, LANES), SIDE + length)
-        total = jnp.zeros((own, length), f32)
-        for v in range(all_cams):
-            left = pltpu.roll(mixed[v, 0:own, earlier], DILATION_STEP, 1)[:, SIDE:]
-            right = pltpu.roll(
-                mixed[v, 2 * own : 3 * own, later], SIDE + length - DILATION_STEP, 1
-            )[:, :length]
-            acc = left + mixed[v, own : 2 * own, centre] + right
-            h = (mixed[v, 3 * own : 4 * own, centre] + jnp.maximum(acc, 0.0)).astype(bf16)
-            mask = coords[v, :, centre].astype(f32)[joints : joints + 1, :]
-            total = total + h.astype(f32) * mask
-        top = total.astype(bf16)
-        rest = (total - top.astype(f32)).astype(bf16)
-        both = jnp.concatenate([top, rest], axis=0)
-        result = lax.dot_general(
-            twice, both, (((0,), (0,)), ((), ())), preferred_element_type=f32
-        ).astype(bf16)
+        tops, rests = [], []
+        for part in range(2):
+            total = jnp.zeros((half, length), f32)
+            for v in range(all_cams):
+                left = pltpu.roll(mixed[v, part, 0:half, earlier], DILATION_STEP, 1)[:, SIDE:]
+                right = pltpu.roll(
+                    mixed[v, part, 2 * half : 3 * half, later], SIDE + length - DILATION_STEP, 1
+                )[:, :length]
+                acc = left + mixed[v, part, half : 2 * half, centre] + right
+                kept = mixed[v, part, 3 * half : 4 * half, centre]
+                h = (kept + jnp.maximum(acc, 0.0)).astype(bf16)
+                mask = coords[v, :, centre].astype(f32)[joints : joints + 1, :]
+                total = total + h.astype(f32) * mask
+            top = total.astype(bf16)
+            tops.append(top)
+            rests.append((total - top.astype(f32)).astype(bf16))
+        both = jnp.concatenate(tops + rests, axis=0)
+        result = jnp.dot(twice, both, preferred_element_type=f32).astype(bf16)
         for p in range(cams):
             part_out[s * cams + p] = result[p * states : (p + 1) * states]
         for p in range(cams):
@@ -485,8 +512,12 @@
 
     for d in range(1, members):
         target = lax.rem(me + d, members)
+        part_copy(target, me, target, part_send.at[target]).wait_send()
+    coord_copy(me, mate, coord_send.at[mate]).wait_send()
+    for a, b in turns:
+        target = alike(a, b, core)
         coord_copy(me, target, coord_send.at[target]).wait_send()
-        part_copy(target, me, target, part_send.at[target]).wait_send()
+        coord_copy(target, mate, relay_send.at[target]).wait_send()
     for d in range(1, count):
         target = lax.rem(i + d, count)
         end_copy(i, target, end_send.at[target]).wait_send()
@@ -522,8 +553,7 @@
         members = group * cams
         all_cams = cams * views
         states = decay_rates.shape[0]
-        first = jnp.pad(expand_weight, ((0, 0), (0, DEPTH - joints), (0, 0)))
-        first = first.reshape(3 * DEPTH, channels).T
+        keys = jnp.transpose(keypoints, (1, 0, 2))
         taps = jnp.transpose(dilated_tap_weight, (1, 0, 2))
         extended = group * length + 2 * SIDE
         dma, vmem, bf16 = (pltpu.SemaphoreType.DMA, pltpu.VMEM, jnp.bfloat16)
@@ -533,14 +563,18 @@
             in_specs=[pl.BlockSpec(memory_space=pltpu.VMEM)] * 6,
             out_specs=pl.BlockSpec(memory_space=pltpu.VMEM),
             scratch_shapes=[
+                vmem((SIDE, channels), jnp.float32),
+                vmem((channels, 3 * DEPTH), bf16),
                 vmem((all_cams, DEPTH, extended), bf16),
                 vmem((all_cams * group + 1, channels, length), bf16),
-                vmem((all_cams, 4 * own, extended), jnp.float32),
+                vmem((all_cams, 2, 2 * own, extended), jnp.float32),
                 vmem((4, layers, rows, channels), bf16),
+                vmem((2 * own, channels), bf16),
                 vmem((DEPTH, length), jnp.float32),
                 vmem((members, states, length), bf16),
                 vmem((members, states, length), bf16),
                 vmem((count, 8, LANES), jnp.float32),
+                dma((members,)),
                 dma((members,)),
                 dma((members,)),
                 dma((members,)),
@@ -556,7 +590,7 @@
             compiler_params=pltpu.CompilerParams(
                 collective_id=0, has_side_effects=True, vmem_limit_bytes=58 * 1024 * 1024
             ),
-        )(keypoints, visibility, first, taps, join_weight, decay_rates)
+        )(keys, visibility, expand_weight, taps, join_weight.T, decay_rates)
 
     return run
 

time: 62.1 us -> 54.4 us (0.88)
  Pallas kernels: 56.8 us -> 52.8 us
  local copies, waits for them, and re-layouts: 5.03 us -> 1.47 us
    pallas_call x1, Pallas kernels: 56.8 us -> 52.8 us  [run(): pl.pallas_call(functools.partial(block_kernel, cams, layers, group), out_...]
    unnamed x7 -> x1, local copies, waits for them, and re-layouts: 3.08 us -> 1.47 us
    reshape x1 -> x0, local copies, waits for them, and re-layouts: 0.99 us -> none  [run(): first = first.reshape(3 * DEPTH, channels).T]
    pad x1 -> x0, local copies, waits for them, and re-layouts: 0.96 us -> none  [run(): first = jnp.pad(expand_weight, ((0, 0), (0, DEPTH - joints), (0, 0)))]
where the time goes in v1:
time: 54.4 us; the launch traced here: 54.3 us
  Pallas kernels  52.8 us (97%)
  local copies, waits for them, and re-layouts  1.47 us (3%)
    pallas_call x1, Pallas kernels, run(): pl.pallas_call(functools.partial(block_kernel, cams, layers, group), out_...  52.8 us
    unnamed x1, local copies, waits for them, and re-layouts  1.47 us

profile of v1, /device:TPU:0, one launch (start us, length us, event | category | flops | bytes accessed | tf_op | source)
XLA Modules:
  0.0 54.3 jit_solution(1017853214169470138)
XLA Ops:
  0.0 52.8 %shard_map.64 = f32[32,512]{1,0:T(8,128)} custom-call(s32[34,2,512]{2,1,0:T(2,128)} %bitcast.4, s32[4,512]{1,0:T(4,128)} %vis_ref.1, bf16[3,34,1024]{2,1,0:T(8,128)(2,1)} %raw_ref.1, bf16[3,64,1024]{2,1,0:T(8,128)(2,1)} %bitcast.3, bf16[64,1024]{1,0:T(8,128)(2,1)} %bitcast.5, f32[32,512]{1,0:T(8,128)} %rates_ref.1), custom_call_target="tpu_custom_call" | custom-call | tf_op jit(solution)/shard_map/pallas_call | solution.py:560
  52.8 1.5 %copy.8 = f32[32,512]{1,0:T(8,128)} copy(f32[32,512]{1,0:T(8,128)} %shard_map.64) | data formatting | bytes 131072

commit v2 on v1

--- a/solution.py
+++ b/solution.py
@@ -132,7 +132,7 @@
 
 def block_kernel(
     cams, layers, group, keys_ref, vis_ref, raw_ref, taps_ref, join_ref, rates_ref, out_ref,
-    first_wide, first_ref, coords, hidden, mixed, weights, stack, stage, part_out, part_in, ends,
+    first_wide, first_ref, coords, hidden, mixed, weights, stack, powers, kept_forms, stage, part_out, part_in, ends,
     coord_send, coord_recv, relay_send, side_send, side_recv, up_send, down_send, tap_recv,
     part_send, part_recv, end_send, end_recv,
 ):
@@ -153,15 +153,33 @@
     me = l * cams + y
 
     barrier = pltpu.get_barrier_semaphore()
-    everyone = cams * count
-    flat = i * cams + y
-
-    @pl.loop(1, everyone)
-    def _(d):
-        other = lax.rem(flat + d, everyone)
-        pl.semaphore_signal(
-            barrier, inc=1, device_id=(other % cams, other // cams), device_id_type=MESH
-        )
+    turns = [(a, b) for a in range(group // 2) for b in range(cams) if a + b > 0]
+    core = l % 2
+    mate = (l + 1 - 2 * core) * cams + y
+
+    def alike(a, b, side):
+        chip = lax.rem(l // 2 + a, group // 2)
+        return (chip * 2 + side) * cams + lax.rem(y + b, cams)
+
+    def greet(cam, tm):
+        pl.semaphore_signal(barrier, inc=1, device_id=(cam, tm), device_id_type=MESH)
+
+    greet(y, z * group + mate // cams)
+    for a, b in turns:
+        target = alike(a, b, core)
+        greet(target % cams, z * group + target // cams)
+
+    @pl.when(z > 0)
+    def _():
+        greet(y, i - group)
+        for p in range(cams):
+            greet(p, z * group - 1)
+
+    @pl.when(z < layers - 1)
+    def _():
+        greet(y, i + group)
+        for p in range(cams):
+            greet(p, (z + 1) * group)
 
     here = pl.ds(pl.multiple_of(SIDE + l * length, LANES), length)
     for v in range(views):
@@ -202,7 +220,13 @@
     ).astype(bf16)
     twice = jnp.concatenate([picked, picked], axis=1)
 
-    pl.semaphore_wait(barrier, everyone - 1)
+    above = 1 - (z + 1) // layers
+    below = (z + layers - 1) // layers
+    ends_layer = above * ((l + 1) // group)
+    begins_layer = below * (1 - (l + group - 1) // group)
+    pl.semaphore_wait(
+        barrier, 1 + len(turns) + above + below + members * (ends_layer + begins_layer)
+    )
 
     def tap_copy(source, target, sem, first):
         src = taps_ref.at[:, pl.ds(pl.multiple_of(y * rows, rows), rows), :]
@@ -270,14 +294,6 @@
     pass_on(z, True, True)
     pass_on(z, False, True)
 
-    turns = [(a, b) for a in range(group // 2) for b in range(cams) if a + b > 0]
-    core = l % 2
-    mate = (l + 1 - 2 * core) * cams + y
-
-    def alike(a, b, side):
-        chip = lax.rem(l // 2 + a, group // 2)
-        return (chip * 2 + side) * cams + lax.rem(y + b, cams)
-
     coord_copy(me, mate, coord_send.at[mate]).start()
     for a, b in turns:
         target = alike(a, b, core)
@@ -295,17 +311,34 @@
 
     lane = lax.broadcasted_iota(jnp.int32, (states, length), 1)
 
-    def scan(prod, values, reverse):
-        step = 1
-        while step < length:
-            turn = length - step if reverse else step
-            fits = (lane < length - step) if reverse else (lane >= step)
-            values = [
-                val + prod * jnp.where(fits, pltpu.roll(val, turn, 1), 0.0) for val in values
-            ]
+    bits = length.bit_length() - 1
+
+    def place(step, reverse):
+        turn = length - step if reverse else step
+        return turn, (lane < length - step) if reverse else (lane >= step)
+
+    def products(prod, reverse):
+        for k in range(bits):
+            powers[int(reverse) * bits + k] = prod
+            turn, fits = place(1 << k, reverse)
             prod = prod * jnp.where(fits, pltpu.roll(prod, turn, 1), 1.0)
-            step *= 2
-        return prod, values
+        return prod
+
+    def scan(value, reverse):
+        for k in range(bits):
+            turn, fits = place(1 << k, reverse)
+            moved = jnp.where(fits, pltpu.roll(value, turn, 1), 0.0)
+            value = value + powers[int(reverse) * bits + k] * moved
+        return value
+
+    rates = rates_ref[...]
+    decay = jnp.exp(-rates)
+    energy = neg_expm1(2.0 * rates)
+    kept_forms[0] = products(decay, False)
+    kept_forms[1] = products(decay, True)
+    kept_forms[2] = scan(energy * kept_forms[0], True)
+    kept_forms[3] = energy
+    kept_forms[4] = jnp.sqrt(energy)
 
     for a, b in turns:
         source = alike(a, b, core)
@@ -340,7 +373,7 @@
         return jnp.maximum(jnp.dot(first_ref[...], x, preferred_element_type=f32), 0.0)
 
     def expand_some(begin, end):
-        @pl.loop(begin, end)
+        @pl.loop(begin, end, unroll=2)
         def _(n):
             v, s = n // group, n % group
             start = pl.multiple_of(SIDE + s * length, LANES)
@@ -376,34 +409,27 @@
         h = jnp.maximum(jnp.dot(first_ref[...], x, preferred_element_type=f32), 0.0)
         hidden[whole, :, v * SIDE : (v + 1) * SIDE] = jnp.where(keep, h, 0.0).astype(bf16)
 
-    rates = rates_ref[...]
-    decay = jnp.exp(-rates)
-    energy = neg_expm1(2.0 * rates)
-    drive = jnp.sqrt(energy)
+    arrive(layers - 1)
+    for part in range(2):
+        stack[pl.ds(part * 2 * own, 2 * own), :] = jnp.concatenate(
+            [weights[o, t] for o in range(4) for t in halves[part]], axis=0
+        )
+    z_slab = jnp.dot(stack[...], hidden[whole], preferred_element_type=f32)
+    z_slab = z_slab.reshape(2, 2 * own, length)
+    for v in range(all_cams):
+        piece = z_slab[:, :, v * SIDE : (v + 1) * SIDE]
+        mixed[v, :, :, 0:SIDE] = piece
+        mixed[v, :, :, SIDE + span : SIDE + span + SIDE] = piece
+
+    @pl.loop(0, whole, unroll=4)
+    def _(n):
+        v, s = n // group, n % group
+        lanes = pl.ds(pl.multiple_of(SIDE + s * length, LANES), length)
+        mixed[v, :, :, lanes] = jnp.dot(
+            stack[...], hidden[n], preferred_element_type=f32
+        ).reshape(2, 2 * own, length)
 
     half = own // 2
-
-    def mix(part):
-        stack[...] = jnp.concatenate(
-            [weights[o, t] for o in range(4) for t in halves[part]], axis=0
-        )
-        z_slab = jnp.dot(stack[...], hidden[whole], preferred_element_type=f32)
-        for v in range(all_cams):
-            piece = z_slab[:, v * SIDE : (v + 1) * SIDE]
-            mixed[v, part, :, 0:SIDE] = piece
-            mixed[v, part, :, SIDE + span : SIDE + span + SIDE] = piece
-
-        @pl.loop(0, whole)
-        def _(n):
-            v, s = n // group, n % group
-            lanes = pl.ds(pl.multiple_of(SIDE + s * length, LANES), length)
-            mixed[v, part, :, lanes] = jnp.dot(
-                stack[...], hidden[n], preferred_element_type=f32
-            )
-
-    mix(0)
-    arrive(layers - 1)
-    mix(1)
 
     def part_copy(slot, source, target, sem):
         return pltpu.make_async_remote_copy(
@@ -462,8 +488,9 @@
         summed = summed + part_in[p].astype(f32)
     joined = summed / jnp.maximum(seen, 1.0)
 
-    prod_fwd, (local,) = scan(decay, [drive * joined], False)
-    prod_back, (back, through) = scan(decay, [energy * local, energy * prod_fwd], True)
+    local = scan(kept_forms[4] * joined, False)
+    back = scan(kept_forms[3] * local, True)
+    prod_fwd, prod_back, through = kept_forms[0], kept_forms[1], kept_forms[2]
 
     square = lax.broadcasted_iota(jnp.int32, (states, LANES), 1)
     packed = jnp.where(
@@ -569,7 +596,9 @@
                 vmem((all_cams * group + 1, channels, length), bf16),
                 vmem((all_cams, 2, 2 * own, extended), jnp.float32),
                 vmem((4, layers, rows, channels), bf16),
-                vmem((2 * own, channels), bf16),
+                vmem((4 * own, channels), bf16),
+                vmem((2 * (length.bit_length() - 1), states, length), jnp.float32),
+                vmem((5, states, length), jnp.float32),
                 vmem((DEPTH, length), jnp.float32),
                 vmem((members, states, length), bf16),
                 vmem((members, states, length), bf16),

time: 54.4 us -> 51.3 us (0.943)
  Pallas kernels: 52.8 us -> 49.7 us
    pallas_call x1, Pallas kernels: 52.8 us -> 49.7 us  [run(): pl.pallas_call(functools.partial(block_kernel, cams, layers, group), out_...]
where the time goes in v2:
time: 51.3 us; the launch traced here: 51.1 us
  Pallas kernels  49.7 us (97%)
  local copies, waits for them, and re-layouts  1.47 us (3%)
    pallas_call x1, Pallas kernels, run(): pl.pallas_call(functools.partial(block_kernel, cams, layers, group), out_...  49.7 us
    unnamed x1, local copies, waits for them, and re-layouts  1.47 us

profile of v2, /device:TPU:0, one launch (start us, length us, event | category | flops | bytes accessed | tf_op | source)
XLA Modules:
  0.0 51.1 jit_solution(13516253178302095250)
XLA Ops:
  0.0 49.7 %shard_map.64 = f32[32,512]{1,0:T(8,128)} custom-call(s32[34,2,512]{2,1,0:T(2,128)} %bitcast.4, s32[4,512]{1,0:T(4,128)} %vis_ref.1, bf16[3,34,1024]{2,1,0:T(8,128)(2,1)} %raw_ref.1, bf16[3,64,1024]{2,1,0:T(8,128)(2,1)} %bitcast.3, bf16[64,1024]{1,0:T(8,128)(2,1)} %bitcast.5, f32[32,512]{1,0:T(8,128)} %rates_ref.1), custom_call_target="tpu_custom_call" | custom-call | tf_op jit(solution)/shard_map/pallas_call | solution.py:587
  49.7 1.5 %copy.8 = f32[32,512]{1,0:T(8,128)} copy(f32[32,512]{1,0:T(8,128)} %shard_map.64) | data formatting | bytes 131072

commit v3 on v2

--- a/solution.py
+++ b/solution.py
@@ -380,10 +380,10 @@
             hidden[n] = expand_block(v, start, length).astype(bf16)
 
     whole = all_cams * group
-    expand_some(0, 3 * whole // 4)
+    expand_some(0, whole // 4)
     for hop in range(2, layers - 1):
         arrive(hop)
-    expand_some(3 * whole // 4, whole)
+    expand_some(whole // 4, whole)
 
     slab = lax.broadcasted_iota(jnp.int32, (DEPTH, SIDE), 1)
     low = slab < SIDE // 2

time: 51.3 us -> 49.4 us (0.963)
  Pallas kernels: 49.7 us -> 47.7 us
    pallas_call x1, Pallas kernels: 49.7 us -> 47.7 us  [run(): pl.pallas_call(functools.partial(block_kernel, cams, layers, group), out_...]
where the time goes in v3:
time: 49.4 us; the launch traced here: 49.2 us
  Pallas kernels  47.7 us (97%)
  local copies, waits for them, and re-layouts  1.47 us (3%)
    pallas_call x1, Pallas kernels, run(): pl.pallas_call(functools.partial(block_kernel, cams, layers, group), out_...  47.7 us
    unnamed x1, local copies, waits for them, and re-layouts  1.47 us

profile of v3, /device:TPU:0, one launch (start us, length us, event | category | flops | bytes accessed | tf_op | source)
XLA Modules:
  0.0 49.2 jit_solution(15849597334214576892)
XLA Ops:
  0.0 47.7 %shard_map.64 = f32[32,512]{1,0:T(8,128)} custom-call(s32[34,2,512]{2,1,0:T(2,128)} %bitcast.4, s32[4,512]{1,0:T(4,128)} %vis_ref.1, bf16[3,34,1024]{2,1,0:T(8,128)(2,1)} %raw_ref.1, bf16[3,64,1024]{2,1,0:T(8,128)(2,1)} %bitcast.3, bf16[64,1024]{1,0:T(8,128)(2,1)} %bitcast.5, f32[32,512]{1,0:T(8,128)} %rates_ref.1), custom_call_target="tpu_custom_call" | custom-call | tf_op jit(solution)/shard_map/pallas_call | solution.py:587
  47.7 1.5 %copy.8 = f32[32,512]{1,0:T(8,128)} copy(f32[32,512]{1,0:T(8,128)} %shard_map.64) | data formatting | bytes 131072
